TPU v7x, 32 devices: a whole 2x2x4 slice. The times are simulated.
32 devices in a mesh: scen: 8 (over z, y), rows: 2 (over x), section: 2 (over core).
Axes of the slice: x: 2, y: 2, z: 4, core: 2. Of those that a mesh axis runs over, the one named last changes fastest.
Arguments:
- lp_blocks: bfloat16 [192, 2, 4, 2, 128, 128], P('scen', 'rows', 'section'), may hold values from -0.1875 to 0.1875
- block_columns: int32 [192, 2, 4, 2], P('scen', None, 'section'), may hold values from 0 to 175
- scenario_nodes: int32 [3, 192], P(None, 'scen'), may hold values from 0 to 511, as said below
- scenario_weights: float32 [192], P('scen'), may hold values from 0.5 to 4.5
- cost: bfloat16 [192, 4, 22528], P('scen', 'section'), may hold values from -6 to 6
- bounds_rhs: float32 [192, 256], P('scen', 'rows'), may hold values from -6 to 6
- primal_start: bfloat16 [192, 4, 22528], P('scen', 'section'), may hold values from 0 to 2
- dual_start: float32 [192, 256], P('scen', 'rows'), may hold values from 0 to 1
- multiplier_start: float32 [192, 4, 512], P('scen', 'section'), may hold values from -3 to 3
- consensus_start: float32 [585, 512], replicated, may hold values from 0 to 2
Outputs:
- primal: float32 [192, 4, 22528], P('scen', 'section')
- dual: float32 [192, 256], P('scen', 'rows')
- multiplier: float32 [192, 4, 512], P('scen', 'section')
- penalty: float32 [], replicated
Inputs may be any that keep to these rules, and one draw needn't show every extreme that they name: `scenario_nodes`: node ids never fall from one scenario to the next at any section; the section-three node is the section-four node // 8 and the section-two node the section-three node // 8; the first scenario lies in node 0 and the last in node 511 of section four.
All inputs are finite; a program needn't handle non-finite values.
Results may differ from a plain program's by a relative error of at most 0.0018.
Values sent between devices are 32-bit elements; how exact they have to be, the bound alone decides.
No kernel may reach another device: no remote copies, remote signals or barrier semaphores. Data moves between devices by JAX's collectives and lax.ppermute only.
A program may use at most 128 MiB of HBM per device.

v0:
```python
import jax
import jax.numpy as jnp
from jax import lax
from jax.sharding import PartitionSpec as P

BLK = 128
CPS = 176
N1 = 8
SWEEPS = 2
N2 = 64
NODES = 585
TAU_STEP = 0.4
SIGMA_STEP = 0.4
RHO_START = 1.0
EPSILON = 1e-06


def averaged(node_table, node_mass):
    positive = node_mass > 0
    safe_mass = jnp.where(positive, node_mass, 1.0)
    return jnp.where(positive[:, None], node_table / safe_mass[:, None], 0.0)


def local(
    lp_blocks,
    block_columns,
    scenario_nodes,
    scenario_weights,
    cost,
    bounds_rhs,
    primal_start,
    dual_start,
    multiplier_start,
    consensus_start,
):
    scenario_count = cost.shape[0]
    local_sections = cost.shape[1]
    columns = cost.shape[2]
    hedged = multiplier_start.shape[2]
    row_blocks = dual_start.shape[1] // BLK
    section_index = lax.axis_index("section")
    row_index = lax.axis_index("rows")
    selector = (block_columns[..., None] == jnp.arange(CPS, dtype=jnp.int32)).astype(jnp.float32)
    local_selector = lax.dynamic_slice_in_dim(
        selector, row_index * row_blocks, row_blocks, 1
    ).astype(jnp.bfloat16)
    offsets = jnp.array([1, 1 + N1, 1 + N1 + N2], jnp.int32)
    node_rows = jnp.concatenate(
        [jnp.zeros((1, scenario_count), jnp.int32), scenario_nodes + offsets[:, None]], axis=0
    )
    local_rows = lax.dynamic_slice_in_dim(
        node_rows, section_index * local_sections, local_sections, 0
    )
    membership = (
        local_rows[:, None, :] == jnp.arange(NODES, dtype=jnp.int32)[None, :, None]
    ).astype(jnp.float32)
    cost_full = cost.astype(jnp.float32)

    def spread(table):
        return jnp.einsum("jns,nc->sjc", membership, table, precision=lax.Precision.HIGHEST)

    penalty = jnp.asarray(RHO_START, jnp.float32)
    primal = primal_start.astype(jnp.float32)
    dual, multiplier, previous = (dual_start, multiplier_start, consensus_start)
    for sweep_index in range(SWEEPS):
        anchors = spread(previous)
        dual_half = dual.reshape(scenario_count, row_blocks, BLK).astype(jnp.bfloat16)
        pieces = jnp.einsum(
            "srjnab,sra->srjnb", lp_blocks, dual_half, preferred_element_type=jnp.float32
        )
        gathered = lax.all_gather(pieces, "rows", axis=1, tiled=True)
        placed = jnp.einsum(
            "srjnc,srjnb->sjcb", selector, gathered, precision=lax.Precision.HIGHEST
        )
        adjoint = placed.reshape(scenario_count, local_sections, columns)
        hedge_term = multiplier + penalty * (primal[:, :, :hedged] - anchors)
        hedge_full = jnp.pad(hedge_term, ((0, 0), (0, 0), (0, columns - hedged)))
        primal_next = jnp.maximum(primal - TAU_STEP * (cost_full + adjoint + hedge_full), 0.0)
        step_half = (2.0 * primal_next - primal).astype(jnp.bfloat16)
        blocks = step_half.reshape(scenario_count, local_sections, CPS, BLK)
        picked = jnp.einsum(
            "srjnc,sjcb->srjnb", local_selector, blocks, preferred_element_type=jnp.float32
        ).astype(jnp.bfloat16)
        image = lax.psum(
            jnp.einsum("srjnab,srjnb->sra", lp_blocks, picked, preferred_element_type=jnp.float32),
            "section",
        )
        dual_next = jnp.maximum(
            dual + SIGMA_STEP * (image.reshape(scenario_count, -1) - bounds_rhs), 0.0
        )
        hedged_next = primal_next[:, :, :hedged]
        weighted = scenario_weights[:, None, None] * hedged_next
        node_table, node_mass = lax.psum(
            (
                jnp.einsum("jns,sjc->nc", membership, weighted, precision=lax.Precision.HIGHEST),
                jnp.einsum(
                    "jns,s->n", membership, scenario_weights, precision=lax.Precision.HIGHEST
                ),
            ),
            "scen",
        )
        consensus = averaged(node_table, node_mass)
        new_anchors = spread(consensus)
        gap_local = jnp.sum(scenario_weights[:, None, None] * (hedged_next - new_anchors) ** 2)
        drift_local = jnp.sum(scenario_weights[:, None, None] * (new_anchors - anchors) ** 2)
        primal_gap, drift_gap = lax.psum((gap_local, drift_local), ("scen", "section"))
        multiplier = multiplier + penalty * (hedged_next - new_anchors)
        penalty = penalty * jnp.sqrt(primal_gap / (drift_gap + EPSILON))
        primal, dual, previous = (primal_next, dual_next, consensus)
    return (primal, dual, multiplier, penalty)


def solution(mesh):
    in_specs = (
        P("scen", "rows", "section", None, None, None),
        P("scen", None, "section", None),
        P(None, "scen"),
        P("scen"),
        P("scen", "section", None),
        P("scen", "rows"),
        P("scen", "section", None),
        P("scen", "rows"),
        P("scen", "section", None),
        P(),
    )
    out_specs = (P("scen", "section", None), P("scen", "rows"), P("scen", "section", None), P())
    return jax.shard_map(local, mesh=mesh, in_specs=in_specs, out_specs=out_specs, check_vma=False)
```

profile of v0, /device:TPU:0, one launch (start us, length us, event | category | flops | bytes accessed | tf_op | source)
XLA Modules:
  0.0 297.4 jit_solution(1320190035164285401)
XLA Ops:
  7.2 0.9 convert_bitcast_fusion.1
  8.1 1.0 copy-done
  9.1 0.5 fusion.14
  9.6 0.1 copy.45
  9.7 5.7 %all-gather = f32[24,4,2,128]{3,0,2,1:T(8,128)S(1)} all-gather(f32[24,2,2,128]{3,0,2,1:T(8,128)S(1)} %bitcast.114), channel_id=2, replica_groups=mesh['scen'=8,'rows'=2,'section'=2] {'rows'}, dimensions={1}, use_global_device_ids=true | all-gather | bytes 147456 | tf_op jit(solution)/shard_map/all_gather | solution.py:71
  15.4 3.8 %fusion.53 = f32[24,2,176,128,1]{3,2,1,0,4:T(8,128)S(1)} fusion(f32[24,2,2,2,128]{4,0,3,2,1:T(8,128)S(1)} %bitcast.113, s32[24,2,2,2]{3,2,0,1:T(2,128)S(1)} %copy.45), kind=kOutput, calls=%fused_computation.58 | convolution fusion | flops 51938304 | bytes 4424448 | tf_op jit(solution)/shard_map/srjnc,srjnb->sjcb/dot_general | solution.py:72
  19.2 2.4 copy.119
  21.6 5.4 %reshape.65 = f32[24,2,22528]{2,0,1:T(8,128)} reshape(f32[24,2,176,128]{3,2,0,1:T(8,128)} %bitcast.103) | data formatting | bytes 8650752 | tf_op jit(solution)/shard_map/reshape | solution.py:75
  26.9 4.4 %copy_convert_fusion = f32[24,2,22528]{2,0,1:T(8,128)} fusion(bf16[24,2,22528]{2,1,0:T(2,128)(2,1)} %param.17), kind=kLoop, calls=%fused_computation.26 | loop fusion | flops 1081344 | bytes 6488064 | tf_op jit(solution)/shard_map/convert_element_type | solution.py:63
  31.3 0.1 broadcast_add_fusion
  31.4 1.9 fusion.50
  33.3 5.4 %subtract_convert_fusion.1 = (bf16[24,2,22528]{2,0,1:T(8,128)(2,1)}, f32[24,2,22528]{2,0,1:T(8,128)S(1)}) fusion(bf16[24,2,22528]{2,1,0:T(2,128)(2,1)} %param.17, f32[24,2,512]{2,0,1:T(8,128)S(1)} %get-tuple-element.29, f32[24,2,22528]{2,0,1:T(8,128)} %reshape.65, bf16[24,2,22528]{2,1,0:T(2,128)(2,1)} %param.15), kind=kLoop, calls=%fused_computation.13 | loop fusion | flops 10813440 | bytes 15237120 | tf_op jit(solution)/shard_map/convert_element_type | solution.py:79
  38.7 2.0 copy-done.1
  40.7 1.8 convolution_bitcast_fusion.1
  42.6 0.2 iota_compare_fusion
  42.8 3.3 %copy.72 = bf16[6,8,176,128]{3,2,1,0:T(8,128)(2,1)} copy(bf16[6,8,176,128]{3,1,2,0:T(8,128)(2,1)} %bitcast.106) | data formatting | bytes 4325376
  46.1 2.3 fusion.40
  48.4 0.9 fusion.12
  49.3 3.3 %psum.66 = f32[24,128]{1,0:T(8,128)S(1)} all-reduce(f32[24,128]{1,0:T(8,128)S(1)} %bitcast.117), channel_id=1, replica_groups=mesh['scen'=8,'rows'=2,'section'=2] {'section'}, use_global_device_ids=true, to_apply=%region_0.1 | all-reduce | flops 3072 | bytes 24576 | tf_op jit(solution)/shard_map/psum | solution.py:84
  52.6 0.5 fusion.10
  53.2 5.1 %all-gather.1 = f32[24,4,2,128]{3,0,2,1:T(8,128)S(1)} all-gather(f32[24,2,2,128]{3,0,2,1:T(8,128)S(1)} %bitcast.115), channel_id=3, replica_groups=mesh['scen'=8,'rows'=2,'section'=2] {'rows'}, dimensions={1}, use_global_device_ids=true | all-gather | bytes 147456 | tf_op jit(solution)/shard_map/all_gather | solution.py:71
  58.3 3.8 %fusion.51 = f32[24,2,176,128,1]{3,2,1,0,4:T(8,128)S(1)} fusion(f32[24,2,2,2,128]{4,0,3,2,1:T(8,128)S(1)} %bitcast.112, s32[24,2,2,2]{3,2,0,1:T(2,128)S(1)} %copy.45), kind=kOutput, calls=%fused_computation.56 | convolution fusion | flops 51938304 | bytes 4424448 | tf_op jit(solution)/shard_map/srjnc,srjnb->sjcb/dot_general | solution.py:72
  62.1 2.4 copy.118
  64.5 5.4 %reshape.70 = f32[24,2,22528]{2,0,1:T(8,128)} reshape(f32[24,2,176,128]{3,2,0,1:T(8,128)} %bitcast.104) | data formatting | bytes 8650752 | tf_op jit(solution)/shard_map/reshape | solution.py:75
  69.9 0.1 convert_reduce_fusion
  70.0 0.2 convolution_reduce_fusion
  70.2 22.1 %psum.67 = f32[585]{0:T(1024)S(1)} all-reduce(f32[585]{0:T(1024)S(1)} %convolution_reduce_fusion), channel_id=1, replica_groups=mesh['scen'=8,'rows'=2,'section'=2] {'scen'}, use_global_device_ids=true, to_apply=%region_2.3 | all-reduce | flops 585 | bytes 4680 | tf_op jit(solution)/shard_map/psum | solution.py:93
  92.2 0.1 iota_compare_fusion.1
  92.3 33.4 %all-reduce.8.cloned.1.call-done = f32[585,512]{1,0:T(8,128)} async-done(((f32[585,512]{1,0:T(8,128)}), f32[585,512]{1,0:T(8,128)}) %all-reduce.8.cloned.1.call-update) | async-done | bytes 1198096 | tf_op jit(solution)/shard_map/psum | solution.py:93
  125.8 2.1 fusion.25
  127.8 1.6 multiply_reduce_fusion.2
  129.4 31.8 %all-reduce.4 = (f32[]{:T(128)}, f32[]{:T(128)}) all-reduce(f32[]{:T(128)} %get-tuple-element.19, f32[]{:T(128)} %get-tuple-element.18), channel_id=1, replica_groups=mesh['scen'=8,'rows'=2,'section'=2] {'scen','section'}, use_global_device_ids=true, to_apply=%region_5.6 | all-reduce | flops 2 | bytes 16 | tf_op jit(solution)/shard_map/psum | solution.py:106
  162.6 0.9 multiply_add_fusion.1
  163.5 5.7 %subtract_convert_fusion = (bf16[24,2,22528]{2,0,1:T(8,128)(2,1)}, f32[24,2,22528]{2,0,1:T(8,128)S(1)}) fusion(f32[24,2,22528]{2,0,1:T(8,128)} %copy-done.1, f32[24,2,512]{2,0,1:T(8,128)S(1)} %multiply_add_fusion.1, f32[24,2,22528]{2,0,1:T(8,128)} %reshape.70, bf16[24,2,22528]{2,1,0:T(2,128)(2,1)} %param.15), kind=kLoop, calls=%fused_computation.12 | loop fusion | flops 9732096 | bytes 17399808 | tf_op jit(solution)/shard_map/convert_element_type | solution.py:79
  169.3 2.0 copy-done.2
  171.3 1.8 convolution_bitcast_fusion
  173.1 7.8 %copy.54 = f32[24,2,22528]{2,1,0:T(2,128)} copy(f32[24,2,22528]{2,0,1:T(8,128)} %copy-done.2) | data formatting | bytes 8650752
  180.9 0.3 copy.73
  181.2 0.6 copy-done.7
  181.8 0.7 fusion.37
  182.5 0.9 fusion.8
  183.4 3.3 %psum.71 = f32[24,128]{1,0:T(8,128)S(1)} all-reduce(f32[24,128]{1,0:T(8,128)S(1)} %bitcast.118), channel_id=1, replica_groups=mesh['scen'=8,'rows'=2,'section'=2] {'section'}, use_global_device_ids=true, to_apply=%region_8.9 | all-reduce | flops 3072 | bytes 24576 | tf_op jit(solution)/shard_map/psum | solution.py:84
  186.7 0.6 add_maximum_fusion
  187.3 64.4 %all-reduce.10.cloned.1.call-done = f32[585,512]{1,0:T(8,128)} async-done(((f32[585,512]{1,0:T(8,128)}), f32[585,512]{1,0:T(8,128)}) %all-reduce.10.cloned.1.call-update) | async-done | bytes 1198096 | tf_op jit(solution)/shard_map/psum | solution.py:93
  251.7 2.1 fusion.22
  253.8 1.7 multiply_reduce_fusion
  255.5 0.7 copy.55
  256.2 31.9 %all-reduce.3 = (f32[]{:T(128)}, f32[]{:T(128)}) all-reduce(f32[]{:T(128)} %get-tuple-element.17, f32[]{:T(128)} %get-tuple-element.16), channel_id=1, replica_groups=mesh['scen'=8,'rows'=2,'section'=2] {'scen','section'}, use_global_device_ids=true, to_apply=%region_11.12 | all-reduce | flops 2 | bytes 16 | tf_op jit(solution)/shard_map/psum | solution.py:106
  (36 shorter events, 0.2 us)
Async XLA Ops:
  7.2 1.9 copy-start
  7.2 2.4 copy-start.12
  7.2 118.6 %all-reduce.8.cloned.1.call-start = ((), (), s32[]{:S(2)}) async-start(), calls=%async_computation | async-start | bytes 2424832 | tf_op jit(solution)/shard_map/psum | solution.py:93
  26.9 4.4 %copy-start.13 = (s32[3,24]{1,0:T(4,128)S(1)}, s32[3,24]{1,0:T(4,128)}, u32[]{:S(2)}) copy-start(s32[3,24]{1,0:T(4,128)} %param.13) | copy-start | bytes 868
  26.9 4.4 %copy-start.14 = (s32[3]{0:T(128)S(1)}, s32[3]{0:T(128)}, u32[]{:S(2)}) copy-start(s32[3]{0:T(128)} %constant.8.clone) | copy-start | bytes 40
  26.9 4.5 %copy-start.4 = (f32[24,2,512]{2,1,0:T(2,128)S(1)}, f32[24,2,512]{2,1,0:T(2,128)}, u32[]{:S(2)}) copy-start(f32[24,2,512]{2,1,0:T(2,128)} %param.19) | copy-start | bytes 294916
  33.3 7.4 %copy-start.10 = (f32[24]{0:T(128)S(1)}, f32[24]{0:T(128)}, u32[]{:S(2)}) copy-start(f32[24]{0:T(128)} %param.14) | copy-start | bytes 292
  38.7 2.0 copy-start.1
  42.5 209.2 %all-reduce.10.cloned.1.call-start = ((), (), s32[]{:S(2)}) async-start(), calls=%async_computation.1 | async-start | bytes 2424832 | tf_op jit(solution)/shard_map/psum | solution.py:93
  42.8 5.6 %copy-start.6 = (pred[24,2,2,2,176]{4,3,2,0,1:T(4,128)(4,1)}, pred[24,2,2,2,176]{4,3,2,0,1:T(4,128)(4,1)S(1)}, u32[]{:S(2)}) copy-start(pred[24,2,2,2,176]{4,3,2,0,1:T(4,128)(4,1)S(1)} %iota_compare_fusion) | copy-start | bytes 101380
  46.1 6.5 %copy-start.5 = (f32[24,128]{1,0:T(8,128)S(1)}, f32[24,128]{1,0:T(8,128)}, u32[]{:S(2)}) copy-start(f32[24,128]{1,0:T(8,128)} %param.18) | copy-start | bytes 36868
  46.1 6.5 %copy-start.8 = (f32[24,128]{1,0:T(8,128)S(1)}, f32[24,128]{1,0:T(8,128)}, u32[]{:S(2)}) copy-start(f32[24,128]{1,0:T(8,128)} %param.16) | copy-start | bytes 36868
  64.5 5.5 %copy-start.11 = (f32[24]{0:T(128)S(1)}, f32[24]{0:T(128)}, u32[]{:S(2)}) copy-start(f32[24]{0:T(128)} %param.14) | copy-start | bytes 292
  169.3 2.0 copy-start.2
  173.1 7.8 %copy-start.3 = (bf16[24,2,22528]{2,0,1:T(8,128)(2,1)S(1)}, bf16[24,2,22528]{2,0,1:T(8,128)(2,1)}, u32[]{:S(2)}) copy-start(bf16[24,2,22528]{2,0,1:T(8,128)(2,1)} %get-tuple-element.24) | copy-start | bytes 6488068
  180.9 0.9 copy-start.7
  181.8 4.9 %copy-start.9 = (f32[24,128]{1,0:T(8,128)S(1)}, f32[24,128]{1,0:T(8,128)}, u32[]{:S(2)}) copy-start(f32[24,128]{1,0:T(8,128)} %param.16) | copy-start | bytes 36868
Sparse Core Ops, SparseCore 0:
  42.7 83.0 all-reduce.7
  173.3 78.4 all-reduce.9
where the time goes:
time: 298 us; the launch traced here: 297 us
  blocking collectives  103 us (35%)
  waiting for transfers between devices  97.9 us (33%)
  local copies, waits for them, and re-layouts  33.3 us (11%)
  matrix products  23.3 us (8%)
  other arithmetic  21.6 us (7%)
  between operations  18.1 us (6%)
    psum x2, waiting for transfers between devices, local(): lax.psum((jnp.einsum('jns,sjc->nc', membership, weighted, precision=lax.P...  97.8 us
    psum x2, blocking collectives, local(): lax.psum((gap_local, drift_local), ('scen', 'section'))  63.7 us
    psum x1, blocking collectives, local(): lax.psum((jnp.einsum('jns,sjc->nc', membership, weighted, precision=lax.P...  22.1 us
    unnamed x35, local copies, waits for them, and re-layouts  17.8 us
    convert_element_type x2, other arithmetic, local(): step_half = (2.0 * primal_next - primal).astype(jnp.bfloat16)  11.1 us
    reshape x2, local copies, waits for them, and re-layouts, local(): adjoint = placed.reshape(scenario_count, local_sections, columns)  10.8 us
    all_gather x2, blocking collectives, local(): gathered = lax.all_gather(pieces, 'rows', axis=1, tiled=True)  10.8 us
    dot_general x2, matrix products, local(): jnp.einsum('srjnc,srjnb->sjcb', selector, gathered, precision=lax.Precisi...  7.67 us
  transfers between devices with their start and end apart: 2, of which 2 were waited for; matrix products, arithmetic and copies ran while one was open for 10% of the time, Pallas kernels for 0%

commit v1 on v0

--- a/solution.py
+++ b/solution.py
@@ -103,7 +103,7 @@
         new_anchors = spread(consensus)
         gap_local = jnp.sum(scenario_weights[:, None, None] * (hedged_next - new_anchors) ** 2)
         drift_local = jnp.sum(scenario_weights[:, None, None] * (new_anchors - anchors) ** 2)
-        primal_gap, drift_gap = lax.psum((gap_local, drift_local), ("scen", "section"))
+        primal_gap, drift_gap = lax.psum(lax.psum((gap_local, drift_local), "scen"), "section")
         multiplier = multiplier + penalty * (hedged_next - new_anchors)
         penalty = penalty * jnp.sqrt(primal_gap / (drift_gap + EPSILON))
         primal, dual, previous = (primal_next, dual_next, consensus)

time: 298 us -> 302 us (1.013)
  waiting for transfers between devices: 97.9 us -> 120 us
  blocking collectives: 103 us -> 83 us
    psum x2, blocking collectives: 63.7 us -> 40.7 us  [local(): lax.psum((gap_local, drift_local), 'scen')]
    psum x2, waiting for transfers between devices: 97.8 us -> 120 us  [local(): lax.psum((jnp.einsum('jns,sjc->nc', membership, weighted, precision=lax.P...]
    unnamed x35 -> x31, local copies, waits for them, and re-layouts: 17.8 us -> 18.4 us
  transfers between devices with their start and end apart: 2 -> 2, of which waited for: 2 -> 2; matrix products, arithmetic and copies ran while one was open for 10% -> 6% of each run, Pallas kernels for 0% -> 0%
where the time goes in v1:
time: 302 us; the launch traced here: 301 us
  waiting for transfers between devices  120 us (40%)
  blocking collectives  83 us (27%)
  local copies, waits for them, and re-layouts  33.9 us (11%)
  matrix products  23.5 us (8%)
  other arithmetic  22.2 us (7%)
  between operations  18 us (6%)
    psum x2, waiting for transfers between devices, local(): lax.psum((jnp.einsum('jns,sjc->nc', membership, weighted, precision=lax.P...  120 us
    psum x2, blocking collectives, local(): lax.psum((gap_local, drift_local), 'scen')  40.7 us
    psum x1, blocking collectives, local(): lax.psum((jnp.einsum('jns,sjc->nc', membership, weighted, precision=lax.P...  22.8 us
    unnamed x31, local copies, waits for them, and re-layouts  18.4 us
    convert_element_type x2, other arithmetic, local(): step_half = (2.0 * primal_next - primal).astype(jnp.bfloat16)  11.1 us
    reshape x2, local copies, waits for them, and re-layouts, local(): adjoint = placed.reshape(scenario_count, local_sections, columns)  10.8 us
    all_gather x2, blocking collectives, local(): gathered = lax.all_gather(pieces, 'rows', axis=1, tiled=True)  10.6 us
    psum x2, blocking collectives, local(): lax.psum(jnp.einsum('srjnab,srjnb->sra', lp_blocks, picked, preferred_ele...  8.92 us
  transfers between devices with their start and end apart: 2, of which 2 were waited for; matrix products, arithmetic and copies ran while one was open for 6% of the time, Pallas kernels for 0%

profile of v1, /device:TPU:0, one launch (start us, length us, event | category | flops | bytes accessed | tf_op | source)
XLA Modules:
  0.0 301.1 jit_solution(3044295252847835743)
XLA Ops:
  7.2 0.9 convert_bitcast_fusion.1
  8.1 1.0 copy-done
  9.1 0.5 fusion.14
  9.6 0.1 copy.45
  9.7 5.7 %all-gather = f32[24,4,2,128]{3,0,2,1:T(8,128)S(1)} all-gather(f32[24,2,2,128]{3,0,2,1:T(8,128)S(1)} %bitcast.114), channel_id=2, replica_groups=mesh['scen'=8,'rows'=2,'section'=2] {'rows'}, dimensions={1}, use_global_device_ids=true | all-gather | bytes 147456 | tf_op jit(solution)/shard_map/all_gather | solution.py:71
  15.4 3.8 %fusion.53 = f32[24,2,176,128,1]{3,2,1,0,4:T(8,128)S(1)} fusion(f32[24,2,2,2,128]{4,0,3,2,1:T(8,128)S(1)} %bitcast.113, s32[24,2,2,2]{3,2,0,1:T(2,128)S(1)} %copy.45), kind=kOutput, calls=%fused_computation.58 | convolution fusion | flops 51938304 | bytes 4424448 | tf_op jit(solution)/shard_map/srjnc,srjnb->sjcb/dot_general | solution.py:72
  19.2 2.4 copy.119
  21.6 5.4 %reshape.65 = f32[24,2,22528]{2,0,1:T(8,128)} reshape(f32[24,2,176,128]{3,2,0,1:T(8,128)} %bitcast.103) | data formatting | bytes 8650752 | tf_op jit(solution)/shard_map/reshape | solution.py:75
  26.9 4.4 %copy_convert_fusion = f32[24,2,22528]{2,0,1:T(8,128)} fusion(bf16[24,2,22528]{2,1,0:T(2,128)(2,1)} %param.17), kind=kLoop, calls=%fused_computation.26 | loop fusion | flops 1081344 | bytes 6488064 | tf_op jit(solution)/shard_map/convert_element_type | solution.py:63
  31.4 1.9 fusion.50
  33.3 5.4 %subtract_convert_fusion.1 = (bf16[24,2,22528]{2,0,1:T(8,128)(2,1)}, f32[24,2,22528]{2,0,1:T(8,128)S(1)}) fusion(bf16[24,2,22528]{2,1,0:T(2,128)(2,1)} %param.17, f32[24,2,512]{2,0,1:T(8,128)S(1)} %get-tuple-element.35, f32[24,2,22528]{2,0,1:T(8,128)} %reshape.65, bf16[24,2,22528]{2,1,0:T(2,128)(2,1)} %param.15), kind=kLoop, calls=%fused_computation.13 | loop fusion | flops 10813440 | bytes 15237120 | tf_op jit(solution)/shard_map/convert_element_type | solution.py:79
  38.7 2.0 copy-done.1
  40.7 1.9 convolution_bitcast_fusion.1
  42.7 0.1 convert_reduce_fusion
  42.8 0.2 convolution_reduce_fusion
  42.9 22.8 %psum.95 = f32[585]{0:T(1024)S(1)} all-reduce(f32[585]{0:T(1024)S(1)} %convolution_reduce_fusion), channel_id=1, replica_groups=mesh['scen'=8,'rows'=2,'section'=2] {'scen'}, use_global_device_ids=true, to_apply=%region_2.3 | all-reduce | flops 585 | bytes 4680 | tf_op jit(solution)/shard_map/psum | solution.py:93
  65.7 3.3 %copy.72 = bf16[6,8,176,128]{3,2,1,0:T(8,128)(2,1)} copy(bf16[6,8,176,128]{3,1,2,0:T(8,128)(2,1)} %bitcast.106) | data formatting | bytes 4325376
  69.0 0.7 iota_compare_fusion.1
  69.7 0.2 iota_compare_fusion
  69.9 0.6 copy-done.6
  70.5 2.4 fusion.40
  72.9 0.9 fusion.12
  73.8 52.0 %all-reduce.10.cloned.1.call-done = f32[585,512]{1,0:T(8,128)} async-done(((f32[585,512]{1,0:T(8,128)}), f32[585,512]{1,0:T(8,128)}) %all-reduce.10.cloned.1.call-update) | async-done | bytes 1198096 | tf_op jit(solution)/shard_map/psum | solution.py:93
  125.8 2.1 fusion.25
  127.9 1.6 multiply_reduce_fusion.2
  129.5 20.4 %all-reduce.4 = (f32[]{:T(128)}, f32[]{:T(128)}) all-reduce(f32[]{:T(128)} %get-tuple-element.19, f32[]{:T(128)} %get-tuple-element.18), channel_id=1, replica_groups=mesh['scen'=8,'rows'=2,'section'=2] {'scen'}, use_global_device_ids=true, to_apply=%region_5.6 | all-reduce | flops 2 | bytes 16 | tf_op jit(solution)/shard_map/psum | solution.py:106
  149.8 4.5 %all-reduce.6 = (f32[24,128]{1,0:T(8,128)S(1)}, f32[]{:T(128)}, f32[]{:T(128)}) all-reduce(f32[24,128]{1,0:T(8,128)S(1)} %bitcast.118, f32[]{:T(128)} %get-tuple-element.22, f32[]{:T(128)} %get-tuple-element.23), channel_id=1, replica_groups=mesh['scen'=8,'rows'=2,'section'=2] {'section'}, use_global_device_ids=true, to_apply=%region_0.1 | all-reduce | flops 3074 | bytes 24592 | tf_op jit(solution)/shard_map/psum | solution.py:84
  155.7 0.5 fusion.10
  156.2 4.9 %all-gather.1 = f32[24,4,2,128]{3,0,2,1:T(8,128)S(1)} all-gather(f32[24,2,2,128]{3,0,2,1:T(8,128)S(1)} %bitcast.115), channel_id=3, replica_groups=mesh['scen'=8,'rows'=2,'section'=2] {'rows'}, dimensions={1}, use_global_device_ids=true | all-gather | bytes 147456 | tf_op jit(solution)/shard_map/all_gather | solution.py:71
  161.1 0.9 multiply_add_fusion.1
  162.1 3.8 %fusion.51 = f32[24,2,176,128,1]{3,2,1,0,4:T(8,128)S(1)} fusion(f32[24,2,2,2,128]{4,0,3,2,1:T(8,128)S(1)} %bitcast.112, s32[24,2,2,2]{3,2,0,1:T(2,128)S(1)} %copy.45), kind=kOutput, calls=%fused_computation.56 | convolution fusion | flops 51938304 | bytes 4424448 | tf_op jit(solution)/shard_map/srjnc,srjnb->sjcb/dot_general | solution.py:72
  165.9 2.4 copy.118
  168.3 5.4 %reshape.70 = f32[24,2,22528]{2,0,1:T(8,128)} reshape(f32[24,2,176,128]{3,2,0,1:T(8,128)} %bitcast.104) | data formatting | bytes 8650752 | tf_op jit(solution)/shard_map/reshape | solution.py:75
  173.7 5.7 %subtract_convert_fusion = (bf16[24,2,22528]{2,0,1:T(8,128)(2,1)}, f32[24,2,22528]{2,0,1:T(8,128)S(1)}) fusion(f32[24,2,22528]{2,0,1:T(8,128)} %copy-done.1, f32[24,2,512]{2,0,1:T(8,128)S(1)} %multiply_add_fusion.1, f32[24,2,22528]{2,0,1:T(8,128)} %reshape.70, bf16[24,2,22528]{2,1,0:T(2,128)(2,1)} %param.15), kind=kLoop, calls=%fused_computation.12 | loop fusion | flops 9732096 | bytes 17399808 | tf_op jit(solution)/shard_map/convert_element_type | solution.py:79
  179.4 2.0 copy-done.2
  181.4 1.8 convolution_bitcast_fusion
  183.2 7.8 %copy.54 = f32[24,2,22528]{2,1,0:T(2,128)} copy(f32[24,2,22528]{2,0,1:T(8,128)} %copy-done.2) | data formatting | bytes 8650752
  191.0 0.3 copy.73
  191.3 0.6 copy-done.7
  191.9 0.7 fusion.37
  192.6 0.9 fusion.8
  193.5 68.4 %all-reduce.12.cloned.1.call-done = f32[585,512]{1,0:T(8,128)} async-done(((f32[585,512]{1,0:T(8,128)}), f32[585,512]{1,0:T(8,128)}) %all-reduce.12.cloned.1.call-update) | async-done | bytes 1198096 | tf_op jit(solution)/shard_map/psum | solution.py:93
  261.9 2.1 fusion.22
  263.9 1.6 multiply_reduce_fusion
  265.6 0.7 copy.55
  266.3 20.4 %all-reduce.3 = (f32[]{:T(128)}, f32[]{:T(128)}) all-reduce(f32[]{:T(128)} %get-tuple-element.17, f32[]{:T(128)} %get-tuple-element.16), channel_id=1, replica_groups=mesh['scen'=8,'rows'=2,'section'=2] {'scen'}, use_global_device_ids=true, to_apply=%region_13.14 | all-reduce | flops 2 | bytes 16 | tf_op jit(solution)/shard_map/psum | solution.py:106
  286.7 4.5 %all-reduce.5 = (f32[24,128]{1,0:T(8,128)S(1)}, f32[]{:T(128)}, f32[]{:T(128)}) all-reduce(f32[24,128]{1,0:T(8,128)S(1)} %bitcast.117, f32[]{:T(128)} %get-tuple-element.20, f32[]{:T(128)} %get-tuple-element.21), channel_id=1, replica_groups=mesh['scen'=8,'rows'=2,'section'=2] {'section'}, use_global_device_ids=true, to_apply=%region_10.11 | all-reduce | flops 3074 | bytes 24592 | tf_op jit(solution)/shard_map/psum | solution.py:84
  292.5 0.6 add_maximum_fusion
  (32 shorter events, 0.3 us)
Async XLA Ops:
  7.2 1.9 copy-start
  7.2 2.4 copy-start.10
  7.2 118.6 %all-reduce.10.cloned.1.call-start = ((), (), s32[]{:S(2)}) async-start(), calls=%async_computation | async-start | bytes 2424832 | tf_op jit(solution)/shard_map/psum | solution.py:93
  26.9 4.4 %copy-start.11 = (s32[3,24]{1,0:T(4,128)S(1)}, s32[3,24]{1,0:T(4,128)}, u32[]{:S(2)}) copy-start(s32[3,24]{1,0:T(4,128)} %param.13) | copy-start | bytes 868
  26.9 4.4 %copy-start.12 = (s32[3]{0:T(128)S(1)}, s32[3]{0:T(128)}, u32[]{:S(2)}) copy-start(s32[3]{0:T(128)} %constant.8.clone) | copy-start | bytes 40
  26.9 4.5 %copy-start.4 = (f32[24,2,512]{2,1,0:T(2,128)S(1)}, f32[24,2,512]{2,1,0:T(2,128)}, u32[]{:S(2)}) copy-start(f32[24,2,512]{2,1,0:T(2,128)} %param.19) | copy-start | bytes 294916
  33.3 7.4 %copy-start.9 = (f32[24]{0:T(128)S(1)}, f32[24]{0:T(128)}, u32[]{:S(2)}) copy-start(f32[24]{0:T(128)} %param.14) | copy-start | bytes 292
  38.7 2.0 copy-start.1
  42.6 219.2 %all-reduce.12.cloned.1.call-start = ((), (), s32[]{:S(2)}) async-start(), calls=%async_computation.1 | async-start | bytes 2424832 | tf_op jit(solution)/shard_map/psum | solution.py:93
  69.9 0.6 copy-start.6
  73.8 81.8 %copy-start.5 = (f32[24,128]{1,0:T(8,128)S(1)}, f32[24,128]{1,0:T(8,128)}, u32[]{:S(2)}) copy-start(f32[24,128]{1,0:T(8,128)} %param.18) | copy-start | bytes 36868
  73.8 81.8 %copy-start.8 = (f32[24,128]{1,0:T(8,128)S(1)}, f32[24,128]{1,0:T(8,128)}, u32[]{:S(2)}) copy-start(f32[24,128]{1,0:T(8,128)} %param.16) | copy-start | bytes 36868
  179.4 2.0 copy-start.2
  183.2 7.8 %copy-start.3 = (bf16[24,2,22528]{2,0,1:T(8,128)(2,1)S(1)}, bf16[24,2,22528]{2,0,1:T(8,128)(2,1)}, u32[]{:S(2)}) copy-start(bf16[24,2,22528]{2,0,1:T(8,128)(2,1)} %get-tuple-element.30) | copy-start | bytes 6488068
  191.0 0.9 copy-start.7
Sparse Core Ops, SparseCore 0:
  42.7 83.0 all-reduce.9
  183.4 78.4 all-reduce.11
